TPU v7x, 512 devices: a whole 4x8x8 slice. The times are simulated.
512 devices in a mesh: rows: 64 (over x, z, core), cols: 8 (over y).
Axes of the slice: x: 4, y: 8, z: 8, core: 2. Of those that a mesh axis runs over, the one named last changes fastest.
Arguments:
- right_sides: float32 [4, 64, 128, 256], P(None, 'rows'), may hold values from -6 to 6
- factor_blocks: bfloat16 [3, 64, 8, 8, 256, 256], P(None, 'rows', 'cols'), may hold values from -0.125 to 0.125
- diag_inverses: bfloat16 [4, 64, 256, 256], P(None, 'rows')
- source_ids: int32 [3, 64, 8, 8], P(None, 'rows', 'cols'), may hold values from 0 to 191, as said below
- block_counts: int32 [3, 64, 8], P(None, 'rows', 'cols'), may hold values from 1 to 8, as said below
Outputs:
- solution: float32 [4, 64, 128, 256], P(None, 'rows', 'cols')
Inputs may be any that keep to these rules, and one draw needn't show every extreme that they name: source_ids[l, t, c, k] = m * 64 + s names a supernode of a level m <= l with s % 8 == c. block_counts[l, t, c] slots of target t on group c hold blocks of the factor; slots at and past it are not part of the factor. In every level some target and group has all 8 slots live.
All inputs are finite; a program needn't handle non-finite values.
Results may differ from a plain program's by a relative error of at most 0.007.
Values may be sent and summed in bfloat16 or wider, within the bound.
A program may use at most 128 MiB of HBM per device.

v0:
```python
import jax
import jax.numpy as jnp
from jax import lax
from jax.sharding import PartitionSpec as P


def locate(source, row_count, col_count):
    return source // row_count * (row_count // col_count) + source % row_count // col_count


def slot_sum(running, blocks, chosen_ids, live_count, solved_store, row_count, col_count):

    def add_block(slot_index, partial_value):
        source = chosen_ids[slot_index]
        solved_piece = lax.dynamic_index_in_dim(
            solved_store, locate(source, row_count, col_count), 0, keepdims=False
        )
        factor_piece = lax.dynamic_index_in_dim(blocks, slot_index, 0, keepdims=False)
        return partial_value + jnp.dot(
            solved_piece, factor_piece, preferred_element_type=jnp.float32
        )

    return lax.fori_loop(0, live_count, add_block, running)


def shards(right_sides, factor_blocks, diag_inverses, source_ids, block_counts):
    row_count = lax.axis_size("rows")
    col_count = lax.axis_size("cols")
    level_count = right_sides.shape[0]
    rhs_count = right_sides.shape[2]
    block_width = right_sides.shape[3]
    share_rows = rhs_count // col_count
    col_index = lax.axis_index("cols")
    per_level = row_count // col_count
    solved_store = jnp.zeros(((level_count - 1) * per_level, rhs_count, block_width), jnp.bfloat16)
    partials = [jnp.zeros((rhs_count, block_width), jnp.float32)] * level_count
    solutions = []
    for level_index in range(level_count):
        if level_index > 0:
            partials[level_index] = slot_sum(
                partials[level_index],
                factor_blocks[level_index - 1, 0, 0],
                source_ids[level_index - 1, 0, 0],
                block_counts[level_index - 1, 0, 0],
                solved_store,
                row_count,
                col_count,
            )
        own_rhs = lax.dynamic_slice_in_dim(
            right_sides[level_index, 0], col_index * share_rows, share_rows, 0
        )
        if level_index > 0:
            own_rhs = own_rhs - lax.psum_scatter(
                partials[level_index], "cols", scatter_dimension=0, tiled=True
            )
        own_solution = jnp.dot(
            own_rhs.astype(jnp.bfloat16),
            diag_inverses[level_index, 0],
            preferred_element_type=jnp.float32,
        )
        solutions.append(own_solution)
        if level_index < level_count - 1:
            pieces = lax.all_gather(
                own_solution.astype(jnp.bfloat16)[None], "rows", axis=0, tiled=True
            )
            grouped = pieces.reshape(per_level, col_count, share_rows, block_width)
            regrouped = lax.all_to_all(grouped, "cols", split_axis=1, concat_axis=2, tiled=True)
            solved_store = solved_store.at[
                level_index * per_level : (level_index + 1) * per_level
            ].set(regrouped[:, 0])
    return jnp.stack(solutions)[:, None]


def solution(mesh):
    return jax.shard_map(
        shards,
        mesh=mesh,
        in_specs=(
            P(None, "rows", None, None),
            P(None, "rows", "cols", None, None, None),
            P(None, "rows", None, None),
            P(None, "rows", "cols", None),
            P(None, "rows", "cols"),
        ),
        out_specs=P(None, "rows", "cols", None),
        check_vma=False,
    )
```

profile of v0, /device:TPU:2, one launch (start us, length us, event | category | flops | bytes accessed | tf_op | source)
XLA Modules:
  0.0 462.0 jit_solution(18360709935676070336)
XLA Ops:
  8.5 56.0 %all-gather = bf16[1024,256]{1,0:T(8,128)(2,1)S(1)} all-gather(bf16[16,256]{1,0:T(8,128)(2,1)S(1)} %get-tuple-element.425), channel_id=2, replica_groups=mesh['rows'=64,'cols'=8] {'rows'}, dimensions={0}, use_global_device_ids=true | all-gather | bytes 532480 | tf_op jit(solution)/shard_map/all_gather | solution.py:63
  65.4 7.1 %all-to-all-start = ((bf16[8,8,16,256]{3,2,0,1:T(8,128)(2,1)}), bf16[8,8,16,256]{3,2,0,1:T(8,128)(2,1)S(1)}, u32[]{:S(2)}, u32[]{:S(2)}) async-start(bf16[8,8,16,256]{3,2,0,1:T(8,128)(2,1)} %copy.11), calls=%async_computation | async-start | bytes 1048576 | tf_op jit(solution)/shard_map/all_to_all | solution.py:67
  73.7 3.5 slice_bitcast_fusion
  77.2 13.3 %all-to-all-done = bf16[8,8,16,256]{3,2,0,1:T(8,128)(2,1)S(1)} async-done(((bf16[8,8,16,256]{3,2,0,1:T(8,128)(2,1)}), bf16[8,8,16,256]{3,2,0,1:T(8,128)(2,1)S(1)}, u32[]{:S(2)}, u32[]{:S(2)}) %all-to-all-start) | async-done | bytes 524320 | tf_op jit(solution)/shard_map/all_to_all | solution.py:67
  90.7 21.3 %while.42 = (s32[]{:T(128)}, f32[128,256]{1,0:T(8,128)S(1)}, s32[]{:T(128)}, s32[8]{0:T(128)S(1)}, bf16[24,128,256]{2,1,0:T(8,128)(2,1)S(1)}, /*index=5*/bf16[8,...) while((s32[]{:T(128)}, f32[128,256]{1,0:T(8,128)S(1)}, ...), condition=%wide.region_1.2_spmd, body=%wide.region_0.0_spmd.sunk | while | flops 16810028 | bytes 459350 | solution.py:23
  94.8 1.1 convolution_add_fusion.6
  100.0 1.1 convolution_add_fusion.6
  105.2 1.1 convolution_add_fusion.6
  110.3 1.1 convolution_add_fusion.6
  112.7 51.3 %reduce-scatter.4.cloned.1.call-done = f32[16,256]{1,0:T(8,128)} async-done(((f32[128,256]{1,0:T(8,128)}), f32[16,256]{1,0:T(8,128)}) %reduce-scatter.4.cloned.1.call-update) | async-done | bytes 16400 | tf_op jit(solution)/shard_map/reduce_scatter | solution.py:53
  164.0 1.1 fusion.41
  165.0 50.9 %all-gather.1 = bf16[1024,256]{1,0:T(8,128)(2,1)S(1)} all-gather(bf16[16,256]{1,0:T(8,128)(2,1)S(1)} %get-tuple-element.427), channel_id=3, replica_groups=mesh['rows'=64,'cols'=8] {'rows'}, dimensions={0}, use_global_device_ids=true | all-gather | bytes 532480 | tf_op jit(solution)/shard_map/all_gather | solution.py:63
  216.7 4.6 all-to-all-start.1
  221.4 18.0 %all-to-all-done.1 = bf16[8,8,16,256]{3,2,0,1:T(8,128)(2,1)S(1)} async-done(((bf16[8,8,16,256]{3,2,0,1:T(8,128)(2,1)}), bf16[8,8,16,256]{3,2,0,1:T(8,128)(2,1)S(1)}, u32[]{:S(2)}, u32[]{:S(2)}) %all-to-all-start.1) | async-done | bytes 524320 | tf_op jit(solution)/shard_map/all_to_all | solution.py:67
  239.4 15.6 %while.43 = (s32[]{:T(128)}, f32[128,256]{1,0:T(8,128)S(1)}, s32[]{:T(128)}, s32[8]{0:T(128)S(1)}, bf16[24,128,256]{2,1,0:T(8,128)(2,1)S(1)}, /*index=5*/bf16[8,...) while((s32[]{:T(128)}, f32[128,256]{1,0:T(8,128)S(1)}, ...), condition=%wide.region_4.5_spmd, body=%wide.region_3.4_spmd.sunk | while | flops 16810028 | bytes 459350 | solution.py:23
  243.3 1.1 convolution_add_fusion.7
  248.3 1.1 convolution_add_fusion.7
  253.3 1.1 convolution_add_fusion.7
  255.7 57.3 %reduce-scatter.6.cloned.1.call-done = f32[16,256]{1,0:T(8,128)} async-done(((f32[128,256]{1,0:T(8,128)}), f32[16,256]{1,0:T(8,128)}) %reduce-scatter.6.cloned.1.call-update) | async-done | bytes 16400 | tf_op jit(solution)/shard_map/reduce_scatter | solution.py:53
  314.1 50.8 %all-gather.2 = bf16[1024,256]{1,0:T(8,128)(2,1)S(1)} all-gather(bf16[16,256]{1,0:T(8,128)(2,1)S(1)} %get-tuple-element.429), channel_id=4, replica_groups=mesh['rows'=64,'cols'=8] {'rows'}, dimensions={0}, use_global_device_ids=true | all-gather | bytes 532480 | tf_op jit(solution)/shard_map/all_gather | solution.py:63
  365.8 4.6 %all-to-all-start.2 = ((bf16[8,8,16,256]{3,2,0,1:T(8,128)(2,1)}), bf16[8,8,16,256]{3,2,0,1:T(8,128)(2,1)S(1)}, u32[]{:S(2)}, u32[]{:S(2)}) async-start(bf16[8,8,16,256]{3,2,0,1:T(8,128)(2,1)} %copy.15), calls=%async_computation.4 | async-start | bytes 1048576 | tf_op jit(solution)/shard_map/all_to_all | solution.py:67
  370.5 18.0 %all-to-all-done.2 = bf16[8,8,16,256]{3,2,0,1:T(8,128)(2,1)S(1)} async-done(((bf16[8,8,16,256]{3,2,0,1:T(8,128)(2,1)}), bf16[8,8,16,256]{3,2,0,1:T(8,128)(2,1)S(1)}, u32[]{:S(2)}, u32[]{:S(2)}) %all-to-all-start.2) | async-done | bytes 524320 | tf_op jit(solution)/shard_map/all_to_all | solution.py:67
  388.6 12.5 %while.44 = (s32[]{:T(128)}, f32[128,256]{1,0:T(8,128)S(1)}, s32[]{:T(128)}, s32[8]{0:T(128)S(1)}, bf16[24,128,256]{2,1,0:T(8,128)(2,1)S(1)}, /*index=5*/bf16[8,...) while((s32[]{:T(128)}, f32[128,256]{1,0:T(8,128)S(1)}, ...), condition=%wide.region_7.8_spmd, body=%wide.region_6.7_spmd.sunk | while | flops 16810028 | bytes 459350 | solution.py:23
  401.8 51.9 %reduce-scatter.8.cloned.1.call-done = f32[16,256]{1,0:T(8,128)} async-done(((f32[128,256]{1,0:T(8,128)}), f32[16,256]{1,0:T(8,128)}) %reduce-scatter.8.cloned.1.call-update) | async-done | bytes 16400 | tf_op jit(solution)/shard_map/reduce_scatter | solution.py:53
  (55 shorter events, 17.9 us)
Async XLA Ops:
  6.5 66.0 %copy-start.4 = (s32[3,1,1]{0,2,1:T(1,128)S(1)}, s32[3,1,1]{0,2,1:T(1,128)}, u32[]{:S(2)}) copy-start(s32[3,1,1]{0,2,1:T(1,128)} %param.21) | copy-start | bytes 40
  6.5 66.6 %copy-start.5 = (s32[3,1,1,8]{3,2,1,0:T(1,128)S(1)}, s32[3,1,1,8]{3,2,1,0:T(1,128)}, u32[]{:S(2)}) copy-start(s32[3,1,1,8]{3,2,1,0:T(1,128)} %param.20) | copy-start | bytes 292
  65.4 25.1 %all-to-all-start = ((bf16[8,8,16,256]{3,2,0,1:T(8,128)(2,1)}), bf16[8,8,16,256]{3,2,0,1:T(8,128)(2,1)S(1)}, u32[]{:S(2)}, u32[]{:S(2)}) async-start(bf16[8,8,16,256]{3,2,0,1:T(8,128)(2,1)} %copy.11), calls=%async_computation | async-start | bytes 1048576 | tf_op jit(solution)/shard_map/all_to_all | solution.py:67
  72.5 91.5 %reduce-scatter.4.cloned.1.call-start = ((), (), s32[]{:S(2)}) async-start(), calls=%async_computation.6 | async-start | bytes 147456 | tf_op jit(solution)/shard_map/reduce_scatter | solution.py:53
  90.7 22.0 %copy-start.3 = (f32[4,1,128,256]{3,2,1,0:T(8,128)S(1)}, f32[4,1,128,256]{3,2,1,0:T(8,128)}, u32[]{:S(2)}) copy-start(f32[4,1,128,256]{3,2,1,0:T(8,128)} %param.17) | copy-start | bytes 1572868
  112.0 0.7 copy-start.1
  216.7 22.7 %copy-start.7 = (s32[8]{0:T(128)S(1)}, s32[8]{0:T(128)}, u32[]{:S(2)}) copy-start(s32[8]{0:T(128)} %get-tuple-element.596) | copy-start | bytes 100
  216.7 22.6 %all-to-all-start.1 = ((bf16[8,8,16,256]{3,2,0,1:T(8,128)(2,1)}), bf16[8,8,16,256]{3,2,0,1:T(8,128)(2,1)S(1)}, u32[]{:S(2)}, u32[]{:S(2)}) async-start(bf16[8,8,16,256]{3,2,0,1:T(8,128)(2,1)} %copy.13), calls=%async_computation.2 | async-start | bytes 1048576 | tf_op jit(solution)/shard_map/all_to_all | solution.py:67
  221.3 91.8 %reduce-scatter.6.cloned.1.call-start = ((), (), s32[]{:S(2)}) async-start(), calls=%async_computation.7 | async-start | bytes 147456 | tf_op jit(solution)/shard_map/reduce_scatter | solution.py:53
  255.1 0.6 copy-start.2
  365.8 22.8 %copy-start.6 = (s32[8]{0:T(128)S(1)}, s32[8]{0:T(128)}, u32[]{:S(2)}) copy-start(s32[8]{0:T(128)} %get-tuple-element.644) | copy-start | bytes 100
  365.8 22.6 %all-to-all-start.2 = ((bf16[8,8,16,256]{3,2,0,1:T(8,128)(2,1)}), bf16[8,8,16,256]{3,2,0,1:T(8,128)(2,1)S(1)}, u32[]{:S(2)}, u32[]{:S(2)}) async-start(bf16[8,8,16,256]{3,2,0,1:T(8,128)(2,1)} %copy.15), calls=%async_computation.4 | async-start | bytes 1048576 | tf_op jit(solution)/shard_map/all_to_all | solution.py:67
  370.4 83.3 %reduce-scatter.8.cloned.1.call-start = ((), (), s32[]{:S(2)}) async-start(), calls=%async_computation.8 | async-start | bytes 147456 | tf_op jit(solution)/shard_map/reduce_scatter | solution.py:53
  401.1 0.6 copy-start
Sparse Core Ops, SparseCore 0:
  112.8 51.1 reduce-scatter.3
  255.9 57.1 reduce-scatter.5
  401.9 51.7 reduce-scatter.7
where the time goes:
time: 464 us; the launch traced here: 462 us
  waiting for transfers between devices  210 us (45%)
  blocking collectives  158 us (34%)
  loops' own time  34.9 us (8%)
  local copies, waits for them, and re-layouts  16.9 us (4%)
  starting transfers between devices  16.4 us (4%)
  between operations  13.3 us (3%)
  matrix products  12.3 us (3%)
    reduce_scatter x3, waiting for transfers between devices, shards(): lax.psum_scatter(partials[level_index], 'cols', scatter_dimension=0, tile...  161 us
    all_gather x3, blocking collectives, shards(): lax.all_gather(own_solution.astype(jnp.bfloat16)[None], 'rows', axis=0, t...  158 us
    all_to_all x3, waiting for transfers between devices, shards(): lax.all_to_all(grouped, 'cols', split_axis=1, concat_axis=2, tiled=True)  49.2 us
    another operation x3, loops' own time, slot_sum(): return lax.fori_loop(0, live_count, add_block, running)  34.9 us
    all_to_all x3, starting transfers between devices, shards(): lax.all_to_all(grouped, 'cols', split_axis=1, concat_axis=2, tiled=True)  16.3 us
  transfers between devices with their start and end apart: 6, of which 6 were waited for; matrix products, arithmetic and copies ran while one was open for 1% of the time, Pallas kernels for 0%

commit v1 on v0

--- a/solution.py
+++ b/solution.py
@@ -2,6 +2,11 @@
 import jax.numpy as jnp
 from jax import lax
 from jax.sharding import PartitionSpec as P
+
+
+def all_by_exchange(shard, name, along):
+    repeated = jnp.stack([shard] * lax.axis_size(name))
+    return jnp.concatenate(lax.all_to_all(repeated, name, 0, 0), axis=along)
 
 
 def locate(source, row_count, col_count):
@@ -60,9 +65,7 @@
         )
         solutions.append(own_solution)
         if level_index < level_count - 1:
-            pieces = lax.all_gather(
-                own_solution.astype(jnp.bfloat16)[None], "rows", axis=0, tiled=True
-            )
+            pieces = all_by_exchange(own_solution.astype(jnp.bfloat16)[None], "rows", 0)
             grouped = pieces.reshape(per_level, col_count, share_rows, block_width)
             regrouped = lax.all_to_all(grouped, "cols", split_axis=1, concat_axis=2, tiled=True)
             solved_store = solved_store.at[

time: 464 us -> 396 us (0.85)
  blocking collectives: 158 us -> 85.5 us
    all_gather x3 -> x0, blocking collectives: 158 us -> none  [shards(): lax.all_gather(own_solution.astype(jnp.bfloat16)[None], 'rows', axis=0, t...]
    all_to_all x0 -> x3, blocking collectives: none -> 85.5 us  [all_by_exchange(): return jnp.concatenate(lax.all_to_all(repeated, name, 0, 0), axis=along)]
where the time goes in v1:
time: 396 us; the launch traced here: 394 us
  waiting for transfers between devices  214 us (54%)
  blocking collectives  85.5 us (22%)
  loops' own time  34.2 us (9%)
  starting transfers between devices  16.1 us (4%)
  local copies, waits for them, and re-layouts  15.5 us (4%)
  matrix products  14.4 us (4%)
  between operations  13.3 us (3%)
    reduce_scatter x3, waiting for transfers between devices, shards(): lax.psum_scatter(partials[level_index], 'cols', scatter_dimension=0, tile...  161 us
    all_to_all x3, blocking collectives, all_by_exchange(): return jnp.concatenate(lax.all_to_all(repeated, name, 0, 0), axis=along)  85.5 us
    all_to_all x3, waiting for transfers between devices, shards(): lax.all_to_all(grouped, 'cols', split_axis=1, concat_axis=2, tiled=True)  52.5 us
    another operation x3, loops' own time, slot_sum(): return lax.fori_loop(0, live_count, add_block, running)  34.2 us
    all_to_all x3, starting transfers between devices, shards(): lax.all_to_all(grouped, 'cols', split_axis=1, concat_axis=2, tiled=True)  16 us
    dot_general x10, matrix products, add_block(): jnp.dot(solved_piece, factor_piece, preferred_element_type=jnp.float32)  10.8 us
  transfers between devices with their start and end apart: 6, of which 6 were waited for; matrix products, arithmetic and copies ran while one was open for 1% of the time, Pallas kernels for 0%

profile of v1, /device:TPU:2, one launch (start us, length us, event | category | flops | bytes accessed | tf_op | source)
XLA Modules:
  0.0 393.7 jit_solution(16068248112014422649)
XLA Ops:
  8.6 30.6 %all_to_all.42 = bf16[64,1,16,256]{3,2,1,0:T(8,128)(2,1)S(1)} all-to-all(bf16[64,1,16,256]{3,2,1,0:T(8,128)(2,1)S(1)} %stack.25), channel_id=1, replica_groups=mesh['rows'=64,'cols'=8] {'rows'}, dimensions={0} | all-to-all | bytes 1048576 | tf_op jit(solution)/shard_map/all_to_all | solution.py:9
  40.0 7.1 %all-to-all-start.1 = ((bf16[8,8,16,256]{3,2,0,1:T(8,128)(2,1)}), bf16[8,8,16,256]{3,2,0,1:T(8,128)(2,1)}, u32[]{:S(2)}, u32[]{:S(2)}) async-start(bf16[8,8,16,256]{3,2,0,1:T(8,128)(2,1)} %copy.11), calls=%async_computation.1 | async-start | bytes 1048576 | tf_op jit(solution)/shard_map/all_to_all | solution.py:70
  47.9 1.7 slice_bitcast_fusion
  49.6 16.0 %all-to-all-done.1 = bf16[8,8,16,256]{3,2,0,1:T(8,128)(2,1)} async-done(((bf16[8,8,16,256]{3,2,0,1:T(8,128)(2,1)}), bf16[8,8,16,256]{3,2,0,1:T(8,128)(2,1)}, u32[]{:S(2)}, u32[]{:S(2)}) %all-to-all-start.1) | async-done | bytes 524320 | tf_op jit(solution)/shard_map/all_to_all | solution.py:70
  66.8 19.2 %while.42 = (s32[]{:T(128)}, f32[128,256]{1,0:T(8,128)S(1)}, s32[]{:T(128)}, s32[8]{0:T(128)S(1)}, bf16[24,128,256]{2,1,0:T(8,128)(2,1)S(1)}, /*index=5*/bf16[8,...) while((s32[]{:T(128)}, f32[128,256]{1,0:T(8,128)S(1)}, ...), condition=%wide.region_1.2_spmd, body=%wide.region_0.0_spmd.sunk | while | flops 16810028 | bytes 459350 | solution.py:28
  70.4 1.1 convolution_add_fusion.6
  75.1 1.1 convolution_add_fusion.6
  79.7 1.1 convolution_add_fusion.6
  84.3 1.1 convolution_add_fusion.6
  86.7 49.0 %reduce-scatter.4.cloned.1.call-done = f32[16,256]{1,0:T(8,128)} async-done(((f32[128,256]{1,0:T(8,128)}), f32[16,256]{1,0:T(8,128)}) %reduce-scatter.4.cloned.1.call-update) | async-done | bytes 16400 | tf_op jit(solution)/shard_map/reduce_scatter | solution.py:58
  136.7 27.4 %all_to_all.43 = bf16[64,1,16,256]{3,2,1,0:T(8,128)(2,1)S(1)} all-to-all(bf16[64,1,16,256]{3,2,1,0:T(8,128)(2,1)S(1)} %stack.27), channel_id=1, replica_groups=mesh['rows'=64,'cols'=8] {'rows'}, dimensions={0} | all-to-all | bytes 1048576 | tf_op jit(solution)/shard_map/all_to_all | solution.py:9
  164.9 4.4 %all-to-all-start.3 = ((bf16[8,8,16,256]{3,2,0,1:T(8,128)(2,1)}), bf16[8,8,16,256]{3,2,0,1:T(8,128)(2,1)S(1)}, u32[]{:S(2)}, u32[]{:S(2)}) async-start(bf16[8,8,16,256]{3,2,0,1:T(8,128)(2,1)} %copy.13), calls=%async_computation.4 | async-start | bytes 1048576 | tf_op jit(solution)/shard_map/all_to_all | solution.py:70
  169.4 18.3 %all-to-all-done.3 = bf16[8,8,16,256]{3,2,0,1:T(8,128)(2,1)S(1)} async-done(((bf16[8,8,16,256]{3,2,0,1:T(8,128)(2,1)}), bf16[8,8,16,256]{3,2,0,1:T(8,128)(2,1)S(1)}, u32[]{:S(2)}, u32[]{:S(2)}) %all-to-all-start.3) | async-done | bytes 524320 | tf_op jit(solution)/shard_map/all_to_all | solution.py:70
  187.8 16.3 %while.43 = (s32[]{:T(128)}, f32[128,256]{1,0:T(8,128)S(1)}, s32[]{:T(128)}, s32[8]{0:T(128)S(1)}, bf16[24,128,256]{2,1,0:T(8,128)(2,1)S(1)}, /*index=5*/bf16[8,...) while((s32[]{:T(128)}, f32[128,256]{1,0:T(8,128)S(1)}, ...), condition=%wide.region_4.5_spmd, body=%wide.region_3.4_spmd.sunk | while | flops 16810028 | bytes 459350 | solution.py:28
  191.9 1.1 convolution_add_fusion.7
  197.2 1.1 convolution_add_fusion.7
  202.4 1.1 convolution_add_fusion.7
  204.8 56.7 %reduce-scatter.6.cloned.1.call-done = f32[16,256]{1,0:T(8,128)} async-done(((f32[128,256]{1,0:T(8,128)}), f32[16,256]{1,0:T(8,128)}) %reduce-scatter.6.cloned.1.call-update) | async-done | bytes 16400 | tf_op jit(solution)/shard_map/reduce_scatter | solution.py:58
  262.5 27.4 %all_to_all.44 = bf16[64,1,16,256]{3,2,1,0:T(8,128)(2,1)S(1)} all-to-all(bf16[64,1,16,256]{3,2,1,0:T(8,128)(2,1)S(1)} %stack.29), channel_id=1, replica_groups=mesh['rows'=64,'cols'=8] {'rows'}, dimensions={0} | all-to-all | bytes 1048576 | tf_op jit(solution)/shard_map/all_to_all | solution.py:9
  290.7 4.4 %all-to-all-start.5 = ((bf16[8,8,16,256]{3,2,0,1:T(8,128)(2,1)}), bf16[8,8,16,256]{3,2,0,1:T(8,128)(2,1)S(1)}, u32[]{:S(2)}, u32[]{:S(2)}) async-start(bf16[8,8,16,256]{3,2,0,1:T(8,128)(2,1)} %copy.15), calls=%async_computation.7 | async-start | bytes 1048576 | tf_op jit(solution)/shard_map/all_to_all | solution.py:70
  295.2 18.3 %all-to-all-done.5 = bf16[8,8,16,256]{3,2,0,1:T(8,128)(2,1)S(1)} async-done(((bf16[8,8,16,256]{3,2,0,1:T(8,128)(2,1)}), bf16[8,8,16,256]{3,2,0,1:T(8,128)(2,1)S(1)}, u32[]{:S(2)}, u32[]{:S(2)}) %all-to-all-start.5) | async-done | bytes 524320 | tf_op jit(solution)/shard_map/all_to_all | solution.py:70
  313.6 15.7 %while.44 = (s32[]{:T(128)}, f32[128,256]{1,0:T(8,128)S(1)}, s32[]{:T(128)}, s32[8]{0:T(128)S(1)}, bf16[24,128,256]{2,1,0:T(8,128)(2,1)S(1)}, /*index=5*/bf16[8,...) while((s32[]{:T(128)}, f32[128,256]{1,0:T(8,128)S(1)}, ...), condition=%wide.region_7.8_spmd, body=%wide.region_6.7_spmd.sunk | while | flops 16810028 | bytes 459350 | solution.py:28
  317.5 1.1 convolution_add_fusion.8
  330.0 55.7 %reduce-scatter.8.cloned.1.call-done = f32[16,256]{1,0:T(8,128)} async-done(((f32[128,256]{1,0:T(8,128)}), f32[16,256]{1,0:T(8,128)}) %reduce-scatter.8.cloned.1.call-update) | async-done | bytes 16400 | tf_op jit(solution)/shard_map/reduce_scatter | solution.py:58
  (58 shorter events, 20.4 us)
Async XLA Ops:
  8.5 38.6 %copy-start.6 = (s32[3,1,1]{0,2,1:T(1,128)S(1)}, s32[3,1,1]{0,2,1:T(1,128)}, u32[]{:S(2)}) copy-start(s32[3,1,1]{0,2,1:T(1,128)} %param.21) | copy-start | bytes 40
  8.6 39.3 %copy-start.7 = (s32[3,1,1,8]{3,2,1,0:T(1,128)S(1)}, s32[3,1,1,8]{3,2,1,0:T(1,128)}, u32[]{:S(2)}) copy-start(s32[3,1,1,8]{3,2,1,0:T(1,128)} %param.20) | copy-start | bytes 292
  8.6 39.3 %copy-start.3 = (bf16[3,1,1,8,256,256]{5,4,3,2,1,0:T(8,128)(2,1)S(1)}, bf16[3,1,1,8,256,256]{5,4,3,2,1,0:T(8,128)(2,1)}, u32[]{:S(2)}) copy-start(bf16[3,1,1,8,256,256]{5,4,3,2,1,0:T(8,128)(2,1)} %param.18) | copy-start | bytes 9437188
  40.0 25.5 %all-to-all-start.1 = ((bf16[8,8,16,256]{3,2,0,1:T(8,128)(2,1)}), bf16[8,8,16,256]{3,2,0,1:T(8,128)(2,1)}, u32[]{:S(2)}, u32[]{:S(2)}) async-start(bf16[8,8,16,256]{3,2,0,1:T(8,128)(2,1)} %copy.11), calls=%async_computation.1 | async-start | bytes 1048576 | tf_op jit(solution)/shard_map/all_to_all | solution.py:70
  47.1 88.6 %reduce-scatter.4.cloned.1.call-start = ((), (), s32[]{:S(2)}) async-start(), calls=%async_computation.9 | async-start | bytes 147456 | tf_op jit(solution)/shard_map/reduce_scatter | solution.py:58
  66.8 19.9 %copy-start.5 = (f32[4,1,128,256]{3,2,1,0:T(8,128)S(1)}, f32[4,1,128,256]{3,2,1,0:T(8,128)}, u32[]{:S(2)}) copy-start(f32[4,1,128,256]{3,2,1,0:T(8,128)} %param.17) | copy-start | bytes 1572868
  66.8 68.9 %copy-start.4 = (bf16[4,1,256,256]{3,2,1,0:T(8,128)(2,1)S(1)}, bf16[4,1,256,256]{3,2,1,0:T(8,128)(2,1)}, u32[]{:S(2)}) copy-start(bf16[4,1,256,256]{3,2,1,0:T(8,128)(2,1)} %param.19) | copy-start | bytes 1572868
  86.0 0.7 copy-start.1
  164.9 22.8 %all-to-all-start.3 = ((bf16[8,8,16,256]{3,2,0,1:T(8,128)(2,1)}), bf16[8,8,16,256]{3,2,0,1:T(8,128)(2,1)S(1)}, u32[]{:S(2)}, u32[]{:S(2)}) async-start(bf16[8,8,16,256]{3,2,0,1:T(8,128)(2,1)} %copy.13), calls=%async_computation.4 | async-start | bytes 1048576 | tf_op jit(solution)/shard_map/all_to_all | solution.py:70
  169.4 92.2 %reduce-scatter.6.cloned.1.call-start = ((), (), s32[]{:S(2)}) async-start(), calls=%async_computation.10 | async-start | bytes 147456 | tf_op jit(solution)/shard_map/reduce_scatter | solution.py:58
  204.1 0.7 copy-start.2
  290.7 22.7 %all-to-all-start.5 = ((bf16[8,8,16,256]{3,2,0,1:T(8,128)(2,1)}), bf16[8,8,16,256]{3,2,0,1:T(8,128)(2,1)S(1)}, u32[]{:S(2)}, u32[]{:S(2)}) async-start(bf16[8,8,16,256]{3,2,0,1:T(8,128)(2,1)} %copy.15), calls=%async_computation.7 | async-start | bytes 1048576 | tf_op jit(solution)/shard_map/all_to_all | solution.py:70
  295.1 90.5 %reduce-scatter.8.cloned.1.call-start = ((), (), s32[]{:S(2)}) async-start(), calls=%async_computation.11 | async-start | bytes 147456 | tf_op jit(solution)/shard_map/reduce_scatter | solution.py:58
  329.3 0.6 copy-start
Sparse Core Ops, SparseCore 0:
  86.8 48.8 reduce-scatter.3
  204.9 56.5 reduce-scatter.5
  330.1 55.5 reduce-scatter.7
